TPU v7x, 32 devices: a whole 2x2x4 slice. The times are simulated.
32 devices in a mesh: groups: 2 (over y), ctx: 4 (over x, core), head: 4 (over z).
Axes of the slice: x: 2, y: 2, z: 4, core: 2. Of those that a mesh axis runs over, the one named last changes fastest.
Arguments:
- context: bfloat16 [8192, 1024], P(('groups', 'ctx', 'head')), parts along dimension 0, may hold values from -6 to 6
- w_kv: bfloat16 [1024, 2048], replicated, may hold values from -0.1875 to 0.1875
- queries: bfloat16 [32, 64, 2048], P(('groups', 'head')), parts along dimension 0, may hold values from -400 to 400
- gain: float32 [1024], replicated, may hold values from 0.25 to 1.75
- w_out: bfloat16 [1024, 1024], P('head'), may hold values from -0.1875 to 0.1875
Outputs:
- latent_out: bfloat16 [4096, 1024], P(('groups', 'ctx', 'head')), parts along dimension 0
There are 2 independent parts, one for each index of `groups`. A program takes and returns all parts, laid end to end along the dimension named above; an argument that names none is the same for every part. Nothing has to cross between parts.
All inputs are finite; a program needn't handle non-finite values.
Results may differ from a plain program's by a relative error of at most 0.01575.
Values may be sent and summed in bfloat16 or wider, within the bound.
No kernel may reach another device: no remote copies, remote signals or barrier semaphores. Data moves between devices by JAX's collectives and lax.ppermute only.
A program may use at most 64 MiB of HBM per device.

v0:
```python
import functools
import math

import jax
import jax.numpy as jnp
from jax import lax
from jax.experimental import pallas as pl
from jax.experimental.pallas import tpu as pltpu
from jax.sharding import PartitionSpec as P


epsilon = 1e-06
stat_rows = 8
f32 = jnp.float32
bf16 = jnp.bfloat16

vmem = pl.BlockSpec(memory_space=pltpu.VMEM)
in_hbm = pl.BlockSpec(memory_space=pltpu.HBM)


def call(kernel, out_shape, args, flops=0, transcendentals=0, scratch=(), in_specs=None):
    moved = sum(math.prod(a.shape) * a.dtype.itemsize for a in args)
    return pl.pallas_call(
        kernel,
        out_shape=out_shape,
        in_specs=in_specs or [vmem] * len(args),
        out_specs=[vmem] * len(out_shape),
        scratch_shapes=list(scratch),
        compiler_params=pltpu.CompilerParams(vmem_limit_bytes=24 << 20),
        cost_estimate=pl.CostEstimate(
            flops=int(flops), transcendentals=int(transcendentals), bytes_accessed=int(moved)
        ),
    )(*args)


def shape(dims, dtype):
    return jax.ShapeDtypeStruct(tuple(dims), dtype)


def partner(value, axis, step):
    count = lax.axis_size(axis)
    return lax.ppermute(value, axis, [(i, i ^ step) for i in range(count)])


def scaled(product, size, scale):
    column = lax.broadcasted_iota(jnp.int32, (1, product.shape[1]), 1)
    factor = jnp.where(lax.rem(column, 2 * size) < size, scale, 1.0).astype(f32)
    return (product * factor).astype(bf16)


def project_first_kernel(steps, size, scale, piece, x_hbm, w_hbm, o_hbm, *refs):
    outs, (x_ref, own_ref, slots, sems, sem) = refs[: len(steps)], refs[len(steps) :]
    width = slots.shape[2]
    here = lax.axis_index("head")
    place = lax.axis_index("groups") * lax.axis_size("ctx") + lax.axis_index("ctx")
    mine = pl.ds(pl.multiple_of(place * piece, piece), piece)
    fetch = pltpu.make_async_copy(x_hbm, x_ref, sem.at[0])
    carry = pltpu.make_async_copy(o_hbm.at[mine, :], own_ref, sem.at[1])
    fetch.start()
    copies = []
    for n, step in enumerate(steps):
        columns = pl.ds(pl.multiple_of((here ^ step) * width, 128), width)
        copies.append(pltpu.make_async_copy(w_hbm.at[:, columns], slots.at[n], sems.at[n]))
        copies[n].start()
    carry.start()
    fetch.wait()
    for n, out_ref in enumerate(outs):
        copies[n].wait()
        product = jnp.dot(x_ref[...], slots[n], preferred_element_type=f32)
        out_ref[...] = scaled(product, size, scale)
    carry.wait()


def project_first(context, w_kv, w_out, steps, size, pieces):
    rows, depth = context.shape
    width = w_kv.shape[1] // lax.axis_size("head")
    piece = w_out.shape[0] // pieces
    return call(
        functools.partial(project_first_kernel, steps, size, 1.0 / math.sqrt(size), piece),
        [shape((rows, width), bf16)] * len(steps)
        + [shape(context.shape, bf16), shape((piece, w_out.shape[1]), bf16)],
        [pltpu.with_memory_space_constraint(a, pltpu.HBM) for a in (context, w_kv, w_out)],
        flops=2 * rows * depth * width * len(steps),
        scratch=[
            pltpu.VMEM((len(steps), depth, width), bf16),
            pltpu.SemaphoreType.DMA((len(steps),)),
            pltpu.SemaphoreType.DMA((2,)),
        ],
        in_specs=[in_hbm] * 3,
    )


def project_kernel(plan, total, size, scale, x_ref, w_ref, *outs):
    here = lax.axis_index("head")
    for (step, first, heads), out_ref in zip(plan, outs):
        start = (here ^ step) * total + 2 * size * first
        columns = pl.ds(pl.multiple_of(start, 128), 2 * size * heads)
        product = jnp.dot(x_ref[...], w_ref[:, columns], preferred_element_type=f32)
        out_ref[...] = scaled(product, size, scale)


def project(context, w_kv, plan, size):
    rows, depth = context.shape
    total = w_kv.shape[1] // lax.axis_size("head")
    return call(
        functools.partial(project_kernel, plan, total, size, 1.0 / math.sqrt(size)),
        [shape((rows, 2 * size * n), bf16) for _, _, n in plan],
        [context, w_kv],
        flops=4 * rows * depth * size * sum(n for _, _, n in plan),
    )


def prepare_kernel(q_ref, out_ref):
    heads, size, _ = q_ref.shape
    for head in range(heads):
        value = q_ref[head].astype(f32) * math.log2(math.e)
        for n in range(3):
            part = value.astype(bf16)
            out_ref[head, n * size : (n + 1) * size, :] = part
            value = value - part.astype(f32)


def prepare(queries):
    heads, size, latents = queries.shape
    (out,) = call(prepare_kernel, [shape((heads, 3 * size, latents), bf16)], [queries])
    return out


def split_stats(top, total):
    rows = []
    for value in (top, total):
        for _ in range(3):
            part = value.astype(bf16).astype(f32)
            rows.append(part)
            value = value - part
    pad = jnp.zeros((stat_rows - len(rows), top.shape[1]), f32)
    return jnp.concatenate(rows + [pad], axis=0).astype(bf16)


def join_stats(block):
    rows = block.astype(f32)
    return rows[0:1] + rows[1:2] + rows[2:3], rows[3:4] + rows[4:5] + rows[5:6]


def attend_kernel(offset, rows, sources, tile, first, last, q_ref, *rest):
    base = 0 if not last else offset
    kv_refs, rest = rest[:sources], rest[sources:]
    if not first:
        (old_ref, old_stat_ref), rest = rest[:2], rest[2:]
    outs, scores_ref = rest[:-1], rest[-1]
    size, latents = q_ref.shape[1] // 3, q_ref.shape[2]
    heads = kv_refs[0].shape[1] // (2 * size)
    blocks = lax.axis_size("ctx")
    block = latents // blocks
    parity = lax.axis_index("ctx") & 1
    parts = block // tile
    work = [
        (head, pair, which, part)
        for head in range(heads)
        for which in range(2)
        for pair in range(blocks // 2)
        for part in range(parts)
    ]
    keys, values = {}, {}

    def lanes_of(item):
        _, pair, which, part = item
        if not last:
            return pl.ds((2 * pair + which) * block + part * tile, tile)
        which = parity if which else 1 - parity
        start = (2 * pair + which) * block + part * tile
        return pl.ds(pl.multiple_of(start, 128), tile)

    def scores(item, slot):
        head = item[0]
        if head not in keys:
            at = 2 * head * size
            keys[head] = [jnp.concatenate([r[0:rows, at : at + size]] * 3, axis=1) for r in kv_refs]
            values[head] = [
                jnp.concatenate(
                    [
                        r[0:rows, at + size : at + 2 * size].astype(f32).T.astype(bf16),
                        jnp.ones((16, rows), bf16),
                    ],
                    axis=0,
                )
                for r in kv_refs
            ]
        query = q_ref[offset + head, :, lanes_of(item)]
        top = None if first else old_stat_ref[base + head, 0:1, lanes_of(item)]
        for i in range(sources):
            s = jnp.dot(keys[head][i], query, preferred_element_type=f32)
            scores_ref[slot, i] = s
            peak = jnp.max(s, axis=0, keepdims=True)
            top = peak if top is None else jnp.maximum(top, peak)
        return top

    def finish(item, slot, top):
        head, pair, which, part = item
        lanes = lanes_of(item)
        if first:
            total, summed = 0.0, 0.0
        else:
            fade = jnp.exp2(old_stat_ref[base + head, 0:1, lanes] - top)
            total = old_stat_ref[base + head, 1:2, lanes] * fade
            summed = old_ref[base + head, :, lanes] * fade
        for i in range(sources):
            weights = jnp.exp2(scores_ref[slot, i] - top)
            product = jnp.dot(values[head][i], weights.astype(bf16), preferred_element_type=f32)
            total += product[size : size + 1]
            summed += product[0:size]
        if not last:
            outs[0][head, :, lanes] = summed
            outs[1][head, 0:1, lanes] = top
            outs[1][head, 1:2, lanes] = total
            return
        at = pl.ds(pair * block + part * tile, tile)
        if which == 0:
            outs[0][head, 0:size, at] = summed.astype(bf16)
            outs[0][head, size:, at] = split_stats(top, total)
        else:
            outs[1][head, :, at] = summed
            outs[2][head, 0:1, at] = top
            outs[2][head, 1:2, at] = total

    top = scores(work[0], 0)
    for n, item in enumerate(work):
        later = scores(work[n + 1], (n + 1) % 2) if n + 1 < len(work) else None
        finish(item, n % 2, top)
        top = later


def attend(queries, parts, state, rows, offset, last):
    size, latents = queries.shape[1] // 3, queries.shape[2]
    heads = parts[0].shape[1] // (2 * size)
    tile = min(512, latents // lax.axis_size("ctx"))
    work = heads * latents * rows * len(parts)
    half = latents // 2
    if last:
        out_shape = [
            shape((heads, size + stat_rows, half), bf16),
            shape((heads, size, half), f32),
            shape((heads, 2, half), f32),
        ]
    else:
        out_shape = [shape((heads, size, latents), f32), shape((heads, 2, latents), f32)]
    return call(
        functools.partial(attend_kernel, offset, rows, len(parts), tile, state is None, last),
        out_shape,
        [queries, *parts, *(state or ())],
        flops=4 * work * size,
        transcendentals=work,
        scratch=[pltpu.VMEM((2, len(parts), rows, tile), f32)],
    )


def merge_kernel(level, last, got_ref, keep_ref, stat_ref, *outs):
    heads, size, lanes = keep_ref.shape
    count = lax.axis_size("ctx") >> level
    others = lax.axis_size("head")
    here = lax.axis_index("head")
    for head in range(heads):

        def merged(at):
            m_got, t_got = join_stats(got_ref[head, size:, at])
            m_own, t_own = stat_ref[head, 0:1, at], stat_ref[head, 1:2, at]
            top = jnp.maximum(m_got, m_own)
            f_got, f_own = jnp.exp2(m_got - top), jnp.exp2(m_own - top)
            total = t_got * f_got + t_own * f_own
            summed = got_ref[head, 0:size, at].astype(f32) * f_got + keep_ref[head, :, at] * f_own
            return summed, top, total

        if last:
            own = lanes // others
            for step in range(others):
                at = pl.ds(pl.multiple_of((here ^ step) * own, 128), own)
                summed, _, total = merged(at)
                outs[step][head] = (summed / total).astype(bf16)
            continue
        send_ref, next_ref, next_stat_ref = outs
        width = lanes // count
        parity = (lax.axis_index("ctx") >> level) & 1
        for pair in range(count // 2):
            to = slice(pair * width, (pair + 1) * width)
            at = pl.ds(pl.multiple_of((2 * pair + 1 - parity) * width, 128), width)
            summed, top, total = merged(at)
            send_ref[head, 0:size, to] = summed.astype(bf16)
            send_ref[head, size:, to] = split_stats(top, total)
            at = pl.ds(pl.multiple_of((2 * pair + parity) * width, 128), width)
            summed, top, total = merged(at)
            next_ref[head, :, to] = summed
            next_stat_ref[head, 0:1, to] = top
            next_stat_ref[head, 1:2, to] = total


def merge(level, got, keep, stat):
    heads, size, lanes = keep.shape
    last = (lax.axis_size("ctx") >> level) == 1
    if last:
        others = lax.axis_size("head")
        out_shape = [shape((heads, size, lanes // others), bf16)] * others
    else:
        out_shape = [
            shape((heads, size + stat_rows, lanes // 2), bf16),
            shape((heads, size, lanes // 2), f32),
            shape((heads, 2, lanes // 2), f32),
        ]
    return call(
        functools.partial(merge_kernel, level, last),
        out_shape,
        [got, keep, stat],
        flops=4 * heads * size * lanes,
    )


def stack_kernel(*refs):
    at = 0
    for ref in refs[:-1]:
        refs[-1][at : at + ref.shape[0]] = ref[...]
        at += ref.shape[0]


def stack(blocks):
    count = sum(b.shape[0] for b in blocks)
    (whole,) = call(stack_kernel, [shape((count,) + blocks[0].shape[1:], bf16)], blocks)
    return whole


def order_kernel(offsets, index, *refs):
    out_ref = refs[-1]
    place = lax.axis_index("groups") * lax.axis_size("ctx") + lax.axis_index("ctx")
    for offset, ref in zip(offsets, refs[:-1]):
        piece = ref.shape[1]
        start = pl.multiple_of((place ^ offset) * piece, piece)
        for i, step in enumerate(index):
            out_ref[step, pl.ds(start, piece), :] = ref[i]


def gather_w_out(own, rows):
    heads, ctx = lax.axis_size("head"), lax.axis_size("ctx")
    piece, columns = own.shape
    held = own.reshape(1, piece, columns)
    index = [0]
    bit = heads // 2
    while bit:
        held = stack([held, partner(held, "head", bit)])
        index = index + [i ^ bit for i in index]
        bit //= 2
    steps = [("ctx", 1 << b, 1 << b) for b in range(1, (ctx - 1).bit_length())]
    steps += [
        ("groups", 1 << b, ctx << b) for b in range((lax.axis_size("groups") - 1).bit_length())
    ]
    steps += [("ctx", 1, 1)]
    offsets = [0]
    held = [held]
    for axis, bit, weight in steps:
        held = held + [partner(h, axis, bit) for h in held]
        offsets = offsets + [o ^ weight for o in offsets]
    (full,) = call(
        functools.partial(order_kernel, offsets, index), [shape((heads, rows, columns), bf16)], held
    )
    return full


def output_kernel(start, width, first, last, *refs):
    count = lax.axis_size("head")
    here = lax.axis_index("head")
    blocks, (gain_ref, w_ref), rest = refs[:count], refs[count : count + 2], refs[count + 2 :]
    heads, size, own = blocks[0].shape
    rows = heads * size
    square = jnp.zeros((1, own), f32) if first else rest[1][...]
    result = jnp.zeros((own, w_ref.shape[2]), f32) if first else rest[0][...]
    for step in range(count):
        block = blocks[step][...].reshape(rows, own).astype(f32)
        square += jnp.sum(block * block, axis=0, keepdims=True)
        gain = gain_ref[here ^ step, :, start : start + rows]
        result += jnp.dot(
            (block.T * gain).astype(bf16),
            w_ref[step, start : start + rows, :],
            preferred_element_type=f32,
        )
    if not last:
        rest[-2][...] = result
        rest[-1][...] = square
        return
    factor = lax.rsqrt(square / width + epsilon)
    factor = jnp.broadcast_to(factor, (128, own)).T[:, 0:1]
    rest[-1][...] = (result * factor).astype(bf16)


def output(blocks, state, start, gain, w_full, last):
    count, rows, columns = w_full.shape
    heads, size, own = blocks[0].shape
    out_shape = [shape((own, columns), bf16)] if last else [
        shape((own, columns), f32), shape((1, own), f32)
    ]
    return call(
        functools.partial(output_kernel, start * size, count * rows, state is None, last),
        out_shape,
        [*blocks, gain.reshape(count, 1, rows), w_full, *(state or ())],
        flops=2 * own * count * heads * size * columns,
    )


def plain_body(context, w_kv, queries, gain, w_out):
    heads_local, head_size, latents = queries.shape
    model_width = w_kv.shape[0]
    total_heads = w_kv.shape[1] // (2 * head_size)
    head_count = lax.axis_size("head")
    ctx_count = lax.axis_size("ctx")
    head_scale = 1.0 / math.sqrt(head_size)
    projected = jnp.dot(context, w_kv, preferred_element_type=jnp.float32).astype(jnp.bfloat16)
    projected = projected.reshape(context.shape[0], total_heads, 2 * head_size)
    regrouped = lax.all_to_all(projected, "head", split_axis=1, concat_axis=0, tiled=True)
    key_rows = regrouped[:, :, :head_size]
    value_rows = regrouped[:, :, head_size:]
    block_size = min(512, latents)
    block_count = latents // block_size
    query_blocks = queries.reshape(heads_local, head_size, block_count, block_size)

    def attend(position):
        query_block = lax.dynamic_index_in_dim(query_blocks, position, 2, keepdims=False)
        scores = (
            jnp.einsum("hdq,khd->hqk", query_block, key_rows, preferred_element_type=jnp.float32)
            * head_scale
        )
        highest = jnp.max(scores, axis=2)
        weights = jnp.exp2(scores - highest[:, :, None])
        row_total = jnp.sum(weights, axis=2)
        summed = jnp.einsum(
            "hqk,khd->hqd",
            weights.astype(jnp.bfloat16),
            value_rows,
            preferred_element_type=jnp.float32,
        )
        return (highest, row_total, summed)

    maxima, totals, partials = lax.map(attend, jnp.arange(block_count))
    maxima = maxima.transpose(1, 0, 2).reshape(heads_local, latents)
    totals = totals.transpose(1, 0, 2).reshape(heads_local, latents)
    partials = partials.transpose(1, 0, 2, 3).reshape(heads_local, latents * head_size // 128, 128)
    ctx_rows = latents // ctx_count
    overall = lax.pmax(maxima, "ctx")
    factor = jnp.exp2(maxima - overall)
    spread = partials.reshape(heads_local, latents, head_size) * factor[:, :, None]
    scaled = spread.reshape(heads_local, latents * head_size // 128, 128)
    sums_own, total_own = (
        lax.psum_scatter(
            scaled.astype(jnp.bfloat16), "ctx", scatter_dimension=1, tiled=True
        ).astype(jnp.float32),
        lax.psum_scatter(
            (totals * factor).astype(jnp.bfloat16), "ctx", scatter_dimension=1, tiled=True
        ).astype(jnp.float32),
    )
    sums_own = sums_own.reshape(heads_local, ctx_rows, head_size)
    attended = sums_own / total_own[:, :, None]
    own_rows = ctx_rows // head_count
    packed = attended.reshape(heads_local, head_count, own_rows * head_size)
    gathered = lax.all_to_all(
        packed.astype(jnp.bfloat16), "head", split_axis=1, concat_axis=0, tiled=True
    ).astype(packed.dtype)
    joined = (
        gathered.reshape(total_heads, own_rows, head_size)
        .transpose(1, 0, 2)
        .reshape(own_rows, model_width)
    )
    mean_square = jnp.sum(joined * joined, axis=1, keepdims=True) / model_width
    normed = (joined * gain[None, :] * lax.rsqrt(mean_square + epsilon)).astype(jnp.bfloat16)
    result = jnp.dot(
        normed,
        lax.all_gather(w_out, "head", axis=0, tiled=True),
        preferred_element_type=jnp.float32,
    )
    return result.astype(jnp.bfloat16)


def fast_shapes(context, queries, w_out):
    heads_local, size, latents = queries.shape
    head_count, ctx_count = lax.axis_size("head"), lax.axis_size("ctx")
    pieces = ctx_count * lax.axis_size("groups")
    powers = (head_count, ctx_count, pieces, size)
    return (
        all(n > 0 and n & (n - 1) == 0 for n in powers)
        and (size.bit_length() - 1) % 2 == 0
        and size % 16 == 0
        and ctx_count > 1
        and head_count > 2
        and heads_local == sum(CHUNKS)
        and (latents // (ctx_count * head_count)) % 128 == 0
        and latents // ctx_count <= 512
        and context.shape[0] % 16 == 0
        and (w_out.shape[0] // pieces) % 16 == 0
    )


def body(context, w_kv, queries, gain, w_out):
    if not fast_shapes(context, queries, w_out):
        return plain_body(context, w_kv, queries, gain, w_out)
    return fast_body(context, w_kv, queries, gain, w_out)


def fast_body(context, w_kv, queries, gain, w_out):
    heads_local, size, _ = queries.shape
    rows = context.shape[0]
    head_count = lax.axis_size("head")
    ctx_count = lax.axis_size("ctx")
    pieces = ctx_count * lax.axis_size("groups")
    starts = [sum(CHUNKS[:n]) for n in range(len(CHUNKS))]
    final = head_count // 2
    far = head_count - 1

    first = [s for s in range(1, head_count) if s != final]
    *sent, near, own = project_first(context, w_kv, w_out, first, size, pieces)
    w_kv, queries, near = lax.optimization_barrier((w_kv, queries, near))
    w_full = gather_w_out(own, w_out.shape[0])
    moved = {s: partner(p, "head", s) for s, p in zip(first, sent)}
    others = [s for s in range(far) if s != final]
    plan = [(0, 0, heads_local)] + [(final, f, n) for f, n in zip(starts, CHUNKS)]
    moved[0], *parts = project(near, w_kv, plan, size)
    late = [partner(p, "head", final) for p in parts]
    queries = prepare(queries)
    state = None
    for s in others + [far]:
        state = attend(queries, [moved[s]], state, rows, 0, False)

    finished = []
    for n in range(len(CHUNKS)):
        sums = attend(queries, [late[n]], state, rows, starts[n], True)
        level = 0
        while (ctx_count >> level) > 1:
            got = partner(sums[0], "ctx", 1 << level)
            level += 1
            sums = merge(level, got, *sums[1:])
        finished.append([partner(sums[s], "head", s) if s else sums[s] for s in range(head_count)])
    state = None
    for n in range(len(CHUNKS)):
        last = n + 1 == len(CHUNKS)
        state = output(finished[n], state, starts[n], gain, w_full, last)
    return state[0]


CHUNKS = [2, 2]


def solution(mesh):
    return jax.shard_map(
        body,
        mesh=mesh,
        in_specs=(
            P(("groups", "ctx", "head"), None),
            P(),
            P(("groups", "head"), None, None),
            P(),
            P("head", None),
        ),
        out_specs=P(("groups", "ctx", "head"), None),
        check_vma=False,
    )
```

profile of v0, /device:TPU:0, one launch (start us, length us, event | category | flops | bytes accessed | tf_op | source)
XLA Modules:
  0.0 73.8 jit_solution(16333996623730806053)
XLA Ops:
  0.0 2.4 %shard_map.55 = (bf16[256,512]{1,0:T(8,128)(2,1)S(1)}, bf16[256,512]{1,0:T(8,128)(2,1)S(1)}, bf16[256,1024]{1,0:T(8,128)(2,1)S(1)}, bf16[32,1024]{1,0:T(8,128)(2,1)S(1)}) custom-call(bf16[256,1024]{1,0:T(8,128)(2,1)} %x_hbm.1, bf16[1024,2048]{1,0:T(8,128)(2,1)} %w_ref, bf16[256,1024]{1,0:T(8,128)(2,1)} %o_hbm.1), custom_call_target="tpu_custom_call" | custom-call | flops 536870912 | bytes 5242880 | tf_op jit(solution)/shard_map/pallas_call | solution.py:23
  2.5 4.1 %collective-permute-start.8 = (bf16[1,32,1024]{2,1,0:T(8,128)(2,1)S(1)}, bf16[1,32,1024]{2,1,0:T(8,128)(2,1)S(1)}, u32[]{:S(2)}, u32[]{:S(2)}) collective-permute-start(bf16[1,32,1024]{2,1,0:T(8,128)(2,1)S(1)} %bitcast.2), channel_id=1, source_target_pairs={{0,2},{1,3},{2,0},{3,1},{4,6},{5,7},{6,4},{7,5},{8,10},{9,11},{10,... | collective-permute-start | bytes 196616 | tf_op jit(solution)/shard_map/ppermute | solution.py:42
  6.6 1.6 %collective-permute-start.2 = (bf16[256,512]{1,0:T(8,128)(2,1)S(1)}, bf16[256,512]{1,0:T(8,128)(2,1)S(1)}, u32[]{:S(2)}, u32[]{:S(2)}) collective-permute-start(bf16[256,512]{1,0:T(8,128)(2,1)S(1)} %get-tuple-element.49), channel_id=1, source_target_pairs={{0,1},{1,0},{2,3},{3,2},{4,5},{5,4},{6,7},{7,6},{8,9},{9,8},{10,11... | collective-permute-start | bytes 786440 | tf_op jit(solution)/shard_map/ppermute | solution.py:42
  8.2 1.5 %collective-permute-done.8.refs_1_ = bf16[1,32,1024]{2,1,0:T(8,128)(2,1)S(1)} collective-permute-done((bf16[1,32,1024]{2,1,0:T(8,128)(2,1)S(1)}, bf16[1,32,1024]{2,1,0:T(8,128)(2,1)S(1)}, u32[]{:S(2)}, u32[]{:S(2)}) %collective-permute-start.8) | collective-permute-done | bytes 65568 | tf_op jit(solution)/shard_map/ppermute | solution.py:42
  9.6 1.9 %collective-permute-start.9 = (bf16[2,32,1024]{2,1,0:T(8,128)(2,1)S(1)}, bf16[2,32,1024]{2,1,0:T(8,128)(2,1)S(1)}, u32[]{:S(2)}, u32[]{:S(2)}) collective-permute-start(bf16[2,32,1024]{2,1,0:T(8,128)(2,1)S(1)} %shard_map.64.refs_0_), channel_id=1, source_target_pairs={{0,1},{1,0},{2,3},{3,2},{4,5},{5,4},{6,7},{7,6},{8,9},{9,8},{10,11... | collective-permute-start | bytes 393224 | tf_op jit(solution)/shard_map/ppermute | solution.py:42
  11.5 2.3 %collective-permute-start.1 = (bf16[256,512]{1,0:T(8,128)(2,1)S(1)}, bf16[256,512]{1,0:T(8,128)(2,1)S(1)}, u32[]{:S(2)}, u32[]{:S(2)}) collective-permute-start(bf16[256,512]{1,0:T(8,128)(2,1)S(1)} %get-tuple-element.48), channel_id=1, source_target_pairs={{0,3},{1,2},{2,1},{3,0},{4,7},{5,6},{6,5},{7,4},{8,11},{9,10},{10,... | collective-permute-start | bytes 786440 | tf_op jit(solution)/shard_map/ppermute | solution.py:42
  13.8 4.2 %collective-permute-done.9.refs_1_ = bf16[2,32,1024]{2,1,0:T(8,128)(2,1)S(1)} collective-permute-done((bf16[2,32,1024]{2,1,0:T(8,128)(2,1)S(1)}, bf16[2,32,1024]{2,1,0:T(8,128)(2,1)S(1)}, u32[]{:S(2)}, u32[]{:S(2)}) %collective-permute-start.9) | collective-permute-done | bytes 131104 | tf_op jit(solution)/shard_map/ppermute | solution.py:42
  18.1 0.0 copy-start.1
  18.1 2.1 %collective-permute-start.10 = (bf16[4,32,1024]{2,1,0:T(8,128)(2,1)S(1)}, bf16[4,32,1024]{2,1,0:T(8,128)(2,1)S(1)}, u32[]{:S(2)}, u32[]{:S(2)}) collective-permute-start(bf16[4,32,1024]{2,1,0:T(8,128)(2,1)S(1)} %shard_map.65.refs_0_), channel_id=1, source_target_pairs={{0,8},{4,12},{8,0},{12,4},{1,9},{5,13},{9,1},{13,5},{2,10},{6,14},... | collective-permute-start | bytes 786440 | tf_op jit(solution)/shard_map/ppermute | solution.py:42
  20.2 0.0 copy-done
  20.2 0.7 shard_map.57
  21.0 1.3 %collective-permute-start.17 = (bf16[256,256]{1,0:T(8,128)(2,1)S(1)}, bf16[256,256]{1,0:T(8,128)(2,1)S(1)}, u32[]{:S(2)}, u32[]{:S(2)}) collective-permute-start(bf16[256,256]{1,0:T(8,128)(2,1)S(1)} %get-tuple-element.68), channel_id=1, source_target_pairs={{0,2},{1,3},{2,0},{3,1},{4,6},{5,7},{6,4},{7,5},{8,10},{9,11},{10,... | collective-permute-start | bytes 393224 | tf_op jit(solution)/shard_map/ppermute | solution.py:42
  22.2 1.7 %collective-permute-start = (bf16[256,256]{1,0:T(8,128)(2,1)S(1)}, bf16[256,256]{1,0:T(8,128)(2,1)S(1)}, u32[]{:S(2)}, u32[]{:S(2)}) collective-permute-start(bf16[256,256]{1,0:T(8,128)(2,1)S(1)} %get-tuple-element.47), channel_id=1, source_target_pairs={{0,2},{1,3},{2,0},{3,1},{4,6},{5,7},{6,4},{7,5},{8,10},{9,11},{10,... | collective-permute-start | bytes 393224 | tf_op jit(solution)/shard_map/ppermute | solution.py:42
  24.0 0.6 shard_map.56.q_ref
  24.6 2.9 %shard_map.58 = (f32[4,64,2048]{2,1,0:T(8,128)S(1)}, f32[4,2,2048]{2,1,0:T(2,128)S(1)}) custom-call(bf16[4,192,2048]{2,1,0:T(8,128)(2,1)S(1)} %shard_map.56.q_ref, bf16[256,512]{1,0:T(8,128)(2,1)S(1)} %get-tuple-element.50.rest_0_), custom_call_target="tpu_custom_call" | custom-call | flops 536870912 | bytes 3407872 | tf_op jit(solution)/shard_map/pallas_call | solution.py:23
  27.5 0.0 collective-permute-done.2.rest_0_
  27.5 3.0 %shard_map.59 = (f32[4,64,2048]{2,1,0:T(8,128)S(1)}, f32[4,2,2048]{2,1,0:T(2,128)S(1)}) custom-call(bf16[4,192,2048]{2,1,0:T(8,128)(2,1)S(1)} %shard_map.56.q_ref, bf16[256,512]{1,0:T(8,128)(2,1)S(1)} %collective-permute-done.2.rest_0_, f32[4,64,2048]{2,1,0:T(8,128)S(1)} %get-tuple-element.51.rest_1_, f32[4,2,2048]{2,1,0:T(2,128)S(1)} %get-tuple-element.52.rest_2_), custom_call_target="tpu_custom_call" | custom-call | flops 536870912 | bytes 5570560 | tf_op jit(solution)/shard_map/pallas_call | solution.py:23
  30.5 0.0 collective-permute-done.1.rest_0_
  30.5 3.0 %shard_map.60 = (f32[4,64,2048]{2,1,0:T(8,128)S(1)}, f32[4,2,2048]{2,1,0:T(2,128)S(1)}) custom-call(bf16[4,192,2048]{2,1,0:T(8,128)(2,1)S(1)} %shard_map.56.q_ref, bf16[256,512]{1,0:T(8,128)(2,1)S(1)} %collective-permute-done.1.rest_0_, f32[4,64,2048]{2,1,0:T(8,128)S(1)} %get-tuple-element.53.rest_1_, f32[4,2,2048]{2,1,0:T(2,128)S(1)} %get-tuple-element.54.rest_2_), custom_call_target="tpu_custom_call" | custom-call | flops 536870912 | bytes 5570560 | tf_op jit(solution)/shard_map/pallas_call | solution.py:23
  33.6 1.9 %collective-permute-done.17.rest_0_ = bf16[256,256]{1,0:T(8,128)(2,1)S(1)} collective-permute-done((bf16[256,256]{1,0:T(8,128)(2,1)S(1)}, bf16[256,256]{1,0:T(8,128)(2,1)S(1)}, u32[]{:S(2)}, u32[]{:S(2)}) %collective-permute-start.17) | collective-permute-done | bytes 131104 | tf_op jit(solution)/shard_map/ppermute | solution.py:42
  35.5 1.7 %shard_map.67 = (bf16[2,72,1024]{2,1,0:T(8,128)(2,1)S(1)}, f32[2,64,1024]{2,1,0:T(8,128)S(1)}, f32[2,2,1024]{2,1,0:T(2,128)S(1)}) custom-call(bf16[4,192,2048]{2,1,0:T(8,128)(2,1)S(1)} %shard_map.56.q_ref, bf16[256,256]{1,0:T(8,128)(2,1)S(1)} %collective-permute-done.17.rest_0_, f32[4,64,2048]{2,1,0:T(8,128)S(1)} %get-tuple-element.55.rest_1_, ...), custom_call_target="tpu_custom_call" | custom-call | flops 268435456 | bytes 5439488 | tf_op jit(solution)/shard_map/pallas_call | solution.py:23
  37.1 0.1 collective-permute-start.18
  37.2 0.0 collective-permute-done.rest_0_
  37.2 1.9 %shard_map.61 = (bf16[2,72,1024]{2,1,0:T(8,128)(2,1)S(1)}, f32[2,64,1024]{2,1,0:T(8,128)S(1)}, f32[2,2,1024]{2,1,0:T(2,128)S(1)}) custom-call(bf16[4,192,2048]{2,1,0:T(8,128)(2,1)S(1)} %shard_map.56.q_ref, bf16[256,256]{1,0:T(8,128)(2,1)S(1)} %collective-permute-done.rest_0_, f32[4,64,2048]{2,1,0:T(8,128)S(1)} %get-tuple-element.55.rest_1_, ...), custom_call_target="tpu_custom_call" | custom-call | flops 268435456 | bytes 5439488 | tf_op jit(solution)/shard_map/pallas_call | solution.py:23
  39.1 0.5 collective-permute-start.3
  39.6 1.5 %collective-permute-start.11 = (bf16[4,32,1024]{2,1,0:T(8,128)(2,1)S(1)}, bf16[4,32,1024]{2,1,0:T(8,128)(2,1)S(1)}, u32[]{:S(2)}, u32[]{:S(2)}) collective-permute-start(bf16[4,32,1024]{2,1,0:T(8,128)(2,1)S(1)} %shard_map.65.refs_0_), channel_id=1, source_target_pairs={{0,16},{16,0},{1,17},{17,1},{2,18},{18,2},{3,19},{19,3},{4,20},{20... | collective-permute-start | bytes 786440 | tf_op jit(solution)/shard_map/ppermute | solution.py:42
  41.1 0.0 collective-permute-done.10.refs_1_
  41.1 0.5 collective-permute-start.12
  41.6 0.0 collective-permute-done.18.got_ref
  41.6 0.2 shard_map.68
  41.8 1.6 %collective-permute-start.19 = (bf16[2,72,512]{2,1,0:T(8,128)(2,1)S(1)}, bf16[2,72,512]{2,1,0:T(8,128)(2,1)S(1)}, u32[]{:S(2)}, u32[]{:S(2)}) collective-permute-start(bf16[2,72,512]{2,1,0:T(8,128)(2,1)S(1)} %get-tuple-element.72), channel_id=1, source_target_pairs={{0,8},{4,12},{8,0},{12,4},{1,9},{5,13},{9,1},{13,5},{2,10},{6,14},... | collective-permute-start | bytes 442376 | tf_op jit(solution)/shard_map/ppermute | solution.py:42
  43.4 0.0 collective-permute-start.13
  43.4 5.4 %collective-permute-done.11.refs_2_ = bf16[4,32,1024]{2,1,0:T(8,128)(2,1)S(1)} collective-permute-done((bf16[4,32,1024]{2,1,0:T(8,128)(2,1)S(1)}, bf16[4,32,1024]{2,1,0:T(8,128)(2,1)S(1)}, u32[]{:S(2)}, u32[]{:S(2)}) %collective-permute-start.11) | collective-permute-done | bytes 262176 | tf_op jit(solution)/shard_map/ppermute | solution.py:42
  48.8 0.0 collective-permute-start.14
  48.8 0.0 collective-permute-done.3.got_ref
  48.8 0.5 collective-permute-start.15
  49.3 4.2 %collective-permute-done.12.refs_3_ = bf16[4,32,1024]{2,1,0:T(8,128)(2,1)S(1)} collective-permute-done((bf16[4,32,1024]{2,1,0:T(8,128)(2,1)S(1)}, bf16[4,32,1024]{2,1,0:T(8,128)(2,1)S(1)}, u32[]{:S(2)}, u32[]{:S(2)}) %collective-permute-start.12) | collective-permute-done | bytes 262176 | tf_op jit(solution)/shard_map/ppermute | solution.py:42
  53.5 0.0 collective-permute-start.16
  53.5 0.2 shard_map.62
  53.7 0.0 collective-permute-done.19.got_ref
  53.7 1.6 %collective-permute-start.4 = (bf16[2,72,512]{2,1,0:T(8,128)(2,1)S(1)}, bf16[2,72,512]{2,1,0:T(8,128)(2,1)S(1)}, u32[]{:S(2)}, u32[]{:S(2)}) collective-permute-start(bf16[2,72,512]{2,1,0:T(8,128)(2,1)S(1)} %get-tuple-element.60), channel_id=1, source_target_pairs={{0,8},{4,12},{8,0},{12,4},{1,9},{5,13},{9,1},{13,5},{2,10},{6,14},... | collective-permute-start | bytes 442376 | tf_op jit(solution)/shard_map/ppermute | solution.py:42
  55.2 0.1 shard_map.69
  55.3 0.0 collective-permute-done.13.refs_4_
  55.3 0.9 %collective-permute-start.20 = (bf16[2,64,128]{2,1,0:T(8,128)(2,1)S(1)}, bf16[2,64,128]{2,1,0:T(8,128)(2,1)S(1)}, u32[]{:S(2)}, u32[]{:S(2)}) collective-permute-start(bf16[2,64,128]{2,1,0:T(8,128)(2,1)S(1)} %get-tuple-element.76), channel_id=1, source_target_pairs={{0,1},{1,0},{2,3},{3,2},{4,5},{5,4},{6,7},{7,6},{8,9},{9,8},{10,11... | collective-permute-start | bytes 98312 | tf_op jit(solution)/shard_map/ppermute | solution.py:42
  56.2 3.8 %collective-permute-done.4.got_ref = bf16[2,72,512]{2,1,0:T(8,128)(2,1)S(1)} collective-permute-done((bf16[2,72,512]{2,1,0:T(8,128)(2,1)S(1)}, bf16[2,72,512]{2,1,0:T(8,128)(2,1)S(1)}, u32[]{:S(2)}, u32[]{:S(2)}) %collective-permute-start.4) | collective-permute-done | bytes 147488 | tf_op jit(solution)/shard_map/ppermute | solution.py:42
  60.0 2.3 %collective-permute-start.21 = (bf16[2,64,128]{2,1,0:T(8,128)(2,1)S(1)}, bf16[2,64,128]{2,1,0:T(8,128)(2,1)S(1)}, u32[]{:S(2)}, u32[]{:S(2)}) collective-permute-start(bf16[2,64,128]{2,1,0:T(8,128)(2,1)S(1)} %get-tuple-element.77), channel_id=1, source_target_pairs={{0,2},{1,3},{2,0},{3,1},{4,6},{5,7},{6,4},{7,5},{8,10},{9,11},{10,... | collective-permute-start | bytes 98312 | tf_op jit(solution)/shard_map/ppermute | solution.py:42
  62.3 0.0 collective-permute-done.14.refs_5_
  62.3 0.9 %collective-permute-start.22 = (bf16[2,64,128]{2,1,0:T(8,128)(2,1)S(1)}, bf16[2,64,128]{2,1,0:T(8,128)(2,1)S(1)}, u32[]{:S(2)}, u32[]{:S(2)}) collective-permute-start(bf16[2,64,128]{2,1,0:T(8,128)(2,1)S(1)} %get-tuple-element.78), channel_id=1, source_target_pairs={{0,3},{1,2},{2,1},{3,0},{4,7},{5,6},{6,5},{7,4},{8,11},{9,10},{10,... | collective-permute-start | bytes 98312 | tf_op jit(solution)/shard_map/ppermute | solution.py:42
  63.2 0.1 shard_map.63
  63.3 0.0 collective-permute-done.15.refs_6_
  63.3 0.3 collective-permute-start.5
  63.7 0.0 collective-permute-done.20.refs_1_
  63.7 3.2 %collective-permute-start.6 = (bf16[2,64,128]{2,1,0:T(8,128)(2,1)S(1)}, bf16[2,64,128]{2,1,0:T(8,128)(2,1)S(1)}, u32[]{:S(2)}, u32[]{:S(2)}) collective-permute-start(bf16[2,64,128]{2,1,0:T(8,128)(2,1)S(1)} %get-tuple-element.65), channel_id=1, source_target_pairs={{0,2},{1,3},{2,0},{3,1},{4,6},{5,7},{6,4},{7,5},{8,10},{9,11},{10,... | collective-permute-start | bytes 98312 | tf_op jit(solution)/shard_map/ppermute | solution.py:42
  66.8 0.0 collective-permute-done.16.refs_7_
  66.8 0.9 %collective-permute-start.7 = (bf16[2,64,128]{2,1,0:T(8,128)(2,1)S(1)}, bf16[2,64,128]{2,1,0:T(8,128)(2,1)S(1)}, u32[]{:S(2)}, u32[]{:S(2)}) collective-permute-start(bf16[2,64,128]{2,1,0:T(8,128)(2,1)S(1)} %get-tuple-element.66), channel_id=1, source_target_pairs={{0,3},{1,2},{2,1},{3,0},{4,7},{5,6},{6,5},{7,4},{8,11},{9,10},{10,... | collective-permute-start | bytes 98312 | tf_op jit(solution)/shard_map/ppermute | solution.py:42
  67.8 0.2 shard_map.66.refs_5_
  67.9 0.0 collective-permute-done.21.refs_2_
  68.0 0.1 collective-permute-done.22.refs_3_
  68.0 0.0 copy-done.2
  68.0 0.5 shard_map.70
  68.5 0.0 collective-permute-done.5.refs_1_
  68.5 0.2 collective-permute-done.6.refs_2_
  68.7 3.8 %collective-permute-done.7.refs_3_ = bf16[2,64,128]{2,1,0:T(8,128)(2,1)S(1)} collective-permute-done((bf16[2,64,128]{2,1,0:T(8,128)(2,1)S(1)}, bf16[2,64,128]{2,1,0:T(8,128)(2,1)S(1)}, u32[]{:S(2)}, u32[]{:S(2)}) %collective-permute-start.7) | collective-permute-done | bytes 32800 | tf_op jit(solution)/shard_map/ppermute | solution.py:42
  72.6 1.2 %shard_map.71 = bf16[128,1024]{1,0:T(8,128)(2,1)} custom-call(bf16[2,64,128]{2,1,0:T(8,128)(2,1)S(1)} %get-tuple-element.63.refs_0_, bf16[2,64,128]{2,1,0:T(8,128)(2,1)S(1)} %collective-permute-done.5.refs_1_, bf16[2,64,128]{2,1,0:T(8,128)(2,1)S(1)} %collective-permute-done.6.refs_2_, bf16[2,64,128]{2,1,0:T(8,128)(2,1)S(1)} %collective-permute-done.7.refs_3_, ...), custom_call_target="tpu_custom_call" | custom-call | flops 134217728 | bytes 2757120 | tf_op jit(solution)/shard_map/pallas_call | solution.py:23
  (5 shorter events, 0.0 us)
Async XLA Ops:
  0.0 20.2 %copy-start = (bf16[1024,2048]{1,0:T(8,128)(2,1)S(1)}, bf16[1024,2048]{1,0:T(8,128)(2,1)}, u32[]{:S(2)}) copy-start(bf16[1024,2048]{1,0:T(8,128)(2,1)} %w_ref) | copy-start | bytes 12582916
  2.5 7.2 %collective-permute-start.8 = (bf16[1,32,1024]{2,1,0:T(8,128)(2,1)S(1)}, bf16[1,32,1024]{2,1,0:T(8,128)(2,1)S(1)}, u32[]{:S(2)}, u32[]{:S(2)}) collective-permute-start(bf16[1,32,1024]{2,1,0:T(8,128)(2,1)S(1)} %bitcast.2), channel_id=1, source_target_pairs={{0,2},{1,3},{2,0},{3,1},{4,6},{5,7},{6,4},{7,5},{8,10},{9,11},{10,... | collective-permute-start | bytes 196616 | tf_op jit(solution)/shard_map/ppermute | solution.py:42
  6.6 20.9 %collective-permute-start.2 = (bf16[256,512]{1,0:T(8,128)(2,1)S(1)}, bf16[256,512]{1,0:T(8,128)(2,1)S(1)}, u32[]{:S(2)}, u32[]{:S(2)}) collective-permute-start(bf16[256,512]{1,0:T(8,128)(2,1)S(1)} %get-tuple-element.49), channel_id=1, source_target_pairs={{0,1},{1,0},{2,3},{3,2},{4,5},{5,4},{6,7},{7,6},{8,9},{9,8},{10,11... | collective-permute-start | bytes 786440 | tf_op jit(solution)/shard_map/ppermute | solution.py:42
  9.6 8.4 %collective-permute-start.9 = (bf16[2,32,1024]{2,1,0:T(8,128)(2,1)S(1)}, bf16[2,32,1024]{2,1,0:T(8,128)(2,1)S(1)}, u32[]{:S(2)}, u32[]{:S(2)}) collective-permute-start(bf16[2,32,1024]{2,1,0:T(8,128)(2,1)S(1)} %shard_map.64.refs_0_), channel_id=1, source_target_pairs={{0,1},{1,0},{2,3},{3,2},{4,5},{5,4},{6,7},{7,6},{8,9},{9,8},{10,11... | collective-permute-start | bytes 393224 | tf_op jit(solution)/shard_map/ppermute | solution.py:42
  11.5 19.0 %collective-permute-start.1 = (bf16[256,512]{1,0:T(8,128)(2,1)S(1)}, bf16[256,512]{1,0:T(8,128)(2,1)S(1)}, u32[]{:S(2)}, u32[]{:S(2)}) collective-permute-start(bf16[256,512]{1,0:T(8,128)(2,1)S(1)} %get-tuple-element.48), channel_id=1, source_target_pairs={{0,3},{1,2},{2,1},{3,0},{4,7},{5,6},{6,5},{7,4},{8,11},{9,10},{10,... | collective-permute-start | bytes 786440 | tf_op jit(solution)/shard_map/ppermute | solution.py:42
  18.1 5.9 %copy-start.1 = (bf16[4,64,2048]{2,1,0:T(8,128)(2,1)S(1)}, bf16[4,64,2048]{2,1,0:T(8,128)(2,1)}, u32[]{:S(2)}) copy-start(bf16[4,64,2048]{2,1,0:T(8,128)(2,1)} %q_ref) | copy-start | bytes 3145732
  18.1 23.0 %collective-permute-start.10 = (bf16[4,32,1024]{2,1,0:T(8,128)(2,1)S(1)}, bf16[4,32,1024]{2,1,0:T(8,128)(2,1)S(1)}, u32[]{:S(2)}, u32[]{:S(2)}) collective-permute-start(bf16[4,32,1024]{2,1,0:T(8,128)(2,1)S(1)} %shard_map.65.refs_0_), channel_id=1, source_target_pairs={{0,8},{4,12},{8,0},{12,4},{1,9},{5,13},{9,1},{13,5},{2,10},{6,14},... | collective-permute-start | bytes 786440 | tf_op jit(solution)/shard_map/ppermute | solution.py:42
  21.0 14.5 %collective-permute-start.17 = (bf16[256,256]{1,0:T(8,128)(2,1)S(1)}, bf16[256,256]{1,0:T(8,128)(2,1)S(1)}, u32[]{:S(2)}, u32[]{:S(2)}) collective-permute-start(bf16[256,256]{1,0:T(8,128)(2,1)S(1)} %get-tuple-element.68), channel_id=1, source_target_pairs={{0,2},{1,3},{2,0},{3,1},{4,6},{5,7},{6,4},{7,5},{8,10},{9,11},{10,... | collective-permute-start | bytes 393224 | tf_op jit(solution)/shard_map/ppermute | solution.py:42
  22.2 15.0 %collective-permute-start = (bf16[256,256]{1,0:T(8,128)(2,1)S(1)}, bf16[256,256]{1,0:T(8,128)(2,1)S(1)}, u32[]{:S(2)}, u32[]{:S(2)}) collective-permute-start(bf16[256,256]{1,0:T(8,128)(2,1)S(1)} %get-tuple-element.47), channel_id=1, source_target_pairs={{0,2},{1,3},{2,0},{3,1},{4,6},{5,7},{6,4},{7,5},{8,10},{9,11},{10,... | collective-permute-start | bytes 393224 | tf_op jit(solution)/shard_map/ppermute | solution.py:42
  37.1 4.5 %collective-permute-start.18 = (bf16[2,72,1024]{2,1,0:T(8,128)(2,1)S(1)}, bf16[2,72,1024]{2,1,0:T(8,128)(2,1)S(1)}, u32[]{:S(2)}, u32[]{:S(2)}) collective-permute-start(bf16[2,72,1024]{2,1,0:T(8,128)(2,1)S(1)} %get-tuple-element.69), channel_id=1, source_target_pairs={{0,4},{4,0},{8,12},{12,8},{1,5},{5,1},{9,13},{13,9},{2,6},{6,2},{1... | collective-permute-start | bytes 884744 | tf_op jit(solution)/shard_map/ppermute | solution.py:42
  39.1 9.7 %collective-permute-start.3 = (bf16[2,72,1024]{2,1,0:T(8,128)(2,1)S(1)}, bf16[2,72,1024]{2,1,0:T(8,128)(2,1)S(1)}, u32[]{:S(2)}, u32[]{:S(2)}) collective-permute-start(bf16[2,72,1024]{2,1,0:T(8,128)(2,1)S(1)} %get-tuple-element.57), channel_id=1, source_target_pairs={{0,4},{4,0},{8,12},{12,8},{1,5},{5,1},{9,13},{13,9},{2,6},{6,2},{1... | collective-permute-start | bytes 884744 | tf_op jit(solution)/shard_map/ppermute | solution.py:42
  39.6 9.2 %collective-permute-start.11 = (bf16[4,32,1024]{2,1,0:T(8,128)(2,1)S(1)}, bf16[4,32,1024]{2,1,0:T(8,128)(2,1)S(1)}, u32[]{:S(2)}, u32[]{:S(2)}) collective-permute-start(bf16[4,32,1024]{2,1,0:T(8,128)(2,1)S(1)} %shard_map.65.refs_0_), channel_id=1, source_target_pairs={{0,16},{16,0},{1,17},{17,1},{2,18},{18,2},{3,19},{19,3},{4,20},{20... | collective-permute-start | bytes 786440 | tf_op jit(solution)/shard_map/ppermute | solution.py:42
  41.1 12.4 %collective-permute-start.12 = (bf16[4,32,1024]{2,1,0:T(8,128)(2,1)S(1)}, bf16[4,32,1024]{2,1,0:T(8,128)(2,1)S(1)}, u32[]{:S(2)}, u32[]{:S(2)}) collective-permute-start(bf16[4,32,1024]{2,1,0:T(8,128)(2,1)S(1)} %collective-permute-done.10.refs_1_), channel_id=1, source_target_pairs={{0,16},{16,0},{1,17},{17,1},{2,18},{18,2},{3,19},{19,3},{4,20},{20... | collective-permute-start | bytes 786440 | tf_op jit(solution)/shard_map/ppermute | solution.py:42
  41.8 11.9 %collective-permute-start.19 = (bf16[2,72,512]{2,1,0:T(8,128)(2,1)S(1)}, bf16[2,72,512]{2,1,0:T(8,128)(2,1)S(1)}, u32[]{:S(2)}, u32[]{:S(2)}) collective-permute-start(bf16[2,72,512]{2,1,0:T(8,128)(2,1)S(1)} %get-tuple-element.72), channel_id=1, source_target_pairs={{0,8},{4,12},{8,0},{12,4},{1,9},{5,13},{9,1},{13,5},{2,10},{6,14},... | collective-permute-start | bytes 442376 | tf_op jit(solution)/shard_map/ppermute | solution.py:42
  43.4 12.0 %collective-permute-start.13 = (bf16[4,32,1024]{2,1,0:T(8,128)(2,1)S(1)}, bf16[4,32,1024]{2,1,0:T(8,128)(2,1)S(1)}, u32[]{:S(2)}, u32[]{:S(2)}) collective-permute-start(bf16[4,32,1024]{2,1,0:T(8,128)(2,1)S(1)} %shard_map.65.refs_0_), channel_id=1, source_target_pairs={{0,4},{4,0},{8,12},{12,8},{1,5},{5,1},{9,13},{13,9},{2,6},{6,2},{1... | collective-permute-start | bytes 786440 | tf_op jit(solution)/shard_map/ppermute | solution.py:42
  48.8 13.5 %collective-permute-start.14 = (bf16[4,32,1024]{2,1,0:T(8,128)(2,1)S(1)}, bf16[4,32,1024]{2,1,0:T(8,128)(2,1)S(1)}, u32[]{:S(2)}, u32[]{:S(2)}) collective-permute-start(bf16[4,32,1024]{2,1,0:T(8,128)(2,1)S(1)} %collective-permute-done.10.refs_1_), channel_id=1, source_target_pairs={{0,4},{4,0},{8,12},{12,8},{1,5},{5,1},{9,13},{13,9},{2,6},{6,2},{1... | collective-permute-start | bytes 786440 | tf_op jit(solution)/shard_map/ppermute | solution.py:42
  48.8 14.5 %collective-permute-start.15 = (bf16[4,32,1024]{2,1,0:T(8,128)(2,1)S(1)}, bf16[4,32,1024]{2,1,0:T(8,128)(2,1)S(1)}, u32[]{:S(2)}, u32[]{:S(2)}) collective-permute-start(bf16[4,32,1024]{2,1,0:T(8,128)(2,1)S(1)} %collective-permute-done.11.refs_2_), channel_id=1, source_target_pairs={{0,4},{4,0},{8,12},{12,8},{1,5},{5,1},{9,13},{13,9},{2,6},{6,2},{1... | collective-permute-start | bytes 786440 | tf_op jit(solution)/shard_map/ppermute | solution.py:42
  53.5 13.3 %collective-permute-start.16 = (bf16[4,32,1024]{2,1,0:T(8,128)(2,1)S(1)}, bf16[4,32,1024]{2,1,0:T(8,128)(2,1)S(1)}, u32[]{:S(2)}, u32[]{:S(2)}) collective-permute-start(bf16[4,32,1024]{2,1,0:T(8,128)(2,1)S(1)} %collective-permute-done.12.refs_3_), channel_id=1, source_target_pairs={{0,4},{4,0},{8,12},{12,8},{1,5},{5,1},{9,13},{13,9},{2,6},{6,2},{1... | collective-permute-start | bytes 786440 | tf_op jit(solution)/shard_map/ppermute | solution.py:42
  53.7 6.3 %collective-permute-start.4 = (bf16[2,72,512]{2,1,0:T(8,128)(2,1)S(1)}, bf16[2,72,512]{2,1,0:T(8,128)(2,1)S(1)}, u32[]{:S(2)}, u32[]{:S(2)}) collective-permute-start(bf16[2,72,512]{2,1,0:T(8,128)(2,1)S(1)} %get-tuple-element.60), channel_id=1, source_target_pairs={{0,8},{4,12},{8,0},{12,4},{1,9},{5,13},{9,1},{13,5},{2,10},{6,14},... | collective-permute-start | bytes 442376 | tf_op jit(solution)/shard_map/ppermute | solution.py:42
  55.3 8.3 %collective-permute-start.20 = (bf16[2,64,128]{2,1,0:T(8,128)(2,1)S(1)}, bf16[2,64,128]{2,1,0:T(8,128)(2,1)S(1)}, u32[]{:S(2)}, u32[]{:S(2)}) collective-permute-start(bf16[2,64,128]{2,1,0:T(8,128)(2,1)S(1)} %get-tuple-element.76), channel_id=1, source_target_pairs={{0,1},{1,0},{2,3},{3,2},{4,5},{5,4},{6,7},{7,6},{8,9},{9,8},{10,11... | collective-permute-start | bytes 98312 | tf_op jit(solution)/shard_map/ppermute | solution.py:42
  60.0 7.9 %collective-permute-start.21 = (bf16[2,64,128]{2,1,0:T(8,128)(2,1)S(1)}, bf16[2,64,128]{2,1,0:T(8,128)(2,1)S(1)}, u32[]{:S(2)}, u32[]{:S(2)}) collective-permute-start(bf16[2,64,128]{2,1,0:T(8,128)(2,1)S(1)} %get-tuple-element.77), channel_id=1, source_target_pairs={{0,2},{1,3},{2,0},{3,1},{4,6},{5,7},{6,4},{7,5},{8,10},{9,11},{10,... | collective-permute-start | bytes 98312 | tf_op jit(solution)/shard_map/ppermute | solution.py:42
  62.3 5.7 %collective-permute-start.22 = (bf16[2,64,128]{2,1,0:T(8,128)(2,1)S(1)}, bf16[2,64,128]{2,1,0:T(8,128)(2,1)S(1)}, u32[]{:S(2)}, u32[]{:S(2)}) collective-permute-start(bf16[2,64,128]{2,1,0:T(8,128)(2,1)S(1)} %get-tuple-element.78), channel_id=1, source_target_pairs={{0,3},{1,2},{2,1},{3,0},{4,7},{5,6},{6,5},{7,4},{8,11},{9,10},{10,... | collective-permute-start | bytes 98312 | tf_op jit(solution)/shard_map/ppermute | solution.py:42
  63.3 5.2 %collective-permute-start.5 = (bf16[2,64,128]{2,1,0:T(8,128)(2,1)S(1)}, bf16[2,64,128]{2,1,0:T(8,128)(2,1)S(1)}, u32[]{:S(2)}, u32[]{:S(2)}) collective-permute-start(bf16[2,64,128]{2,1,0:T(8,128)(2,1)S(1)} %get-tuple-element.64), channel_id=1, source_target_pairs={{0,1},{1,0},{2,3},{3,2},{4,5},{5,4},{6,7},{7,6},{8,9},{9,8},{10,11... | collective-permute-start | bytes 98312 | tf_op jit(solution)/shard_map/ppermute | solution.py:42
  63.7 5.1 %collective-permute-start.6 = (bf16[2,64,128]{2,1,0:T(8,128)(2,1)S(1)}, bf16[2,64,128]{2,1,0:T(8,128)(2,1)S(1)}, u32[]{:S(2)}, u32[]{:S(2)}) collective-permute-start(bf16[2,64,128]{2,1,0:T(8,128)(2,1)S(1)} %get-tuple-element.65), channel_id=1, source_target_pairs={{0,2},{1,3},{2,0},{3,1},{4,6},{5,7},{6,4},{7,5},{8,10},{9,11},{10,... | collective-permute-start | bytes 98312 | tf_op jit(solution)/shard_map/ppermute | solution.py:42
  66.8 1.2 %copy-start.2 = (f32[1024]{0:T(1024)S(1)}, f32[1024]{0:T(1024)}, u32[]{:S(2)}) copy-start(f32[1024]{0:T(1024)} %param.8) | copy-start | bytes 12292
  66.8 5.7 %collective-permute-start.7 = (bf16[2,64,128]{2,1,0:T(8,128)(2,1)S(1)}, bf16[2,64,128]{2,1,0:T(8,128)(2,1)S(1)}, u32[]{:S(2)}, u32[]{:S(2)}) collective-permute-start(bf16[2,64,128]{2,1,0:T(8,128)(2,1)S(1)} %get-tuple-element.66), channel_id=1, source_target_pairs={{0,3},{1,2},{2,1},{3,0},{4,7},{5,6},{6,5},{7,4},{8,11},{9,10},{10,... | collective-permute-start | bytes 98312 | tf_op jit(solution)/shard_map/ppermute | solution.py:42
where the time goes:
time: 73.9 us; the launch traced here: 73.8 us
  starting transfers between devices  29.8 us (40%)
  waiting for transfers between devices  25.2 us (34%)
  Pallas kernels  18.6 us (25%)
    ppermute x23, starting transfers between devices, partner(): return lax.ppermute(value, axis, [(i, i ^ step) for i in range(count)])  29.8 us
    ppermute x23, waiting for transfers between devices, partner(): return lax.ppermute(value, axis, [(i, i ^ step) for i in range(count)])  25.2 us
    pallas_call x17, Pallas kernels, call(): pl.pallas_call(kernel, out_shape=out_shape, in_specs=in_specs or [vmem] *...  18.6 us
  transfers between devices with their start and end apart: 23, of which 9 were waited for; matrix products, arithmetic and copies ran while one was open for 0% of the time, Pallas kernels for 20%

commit v1 on v0

--- a/solution.py
+++ b/solution.py
@@ -362,16 +362,16 @@
     return full
 
 
-def output_kernel(start, width, first, last, *refs):
-    count = lax.axis_size("head")
+def output_kernel(start, width, steps, first, last, *refs):
+    count = len(steps)
     here = lax.axis_index("head")
     blocks, (gain_ref, w_ref), rest = refs[:count], refs[count : count + 2], refs[count + 2 :]
     heads, size, own = blocks[0].shape
     rows = heads * size
     square = jnp.zeros((1, own), f32) if first else rest[1][...]
     result = jnp.zeros((own, w_ref.shape[2]), f32) if first else rest[0][...]
-    for step in range(count):
-        block = blocks[step][...].reshape(rows, own).astype(f32)
+    for step, block_ref in zip(steps, blocks):
+        block = block_ref[...].reshape(rows, own).astype(f32)
         square += jnp.sum(block * block, axis=0, keepdims=True)
         gain = gain_ref[here ^ step, :, start : start + rows]
         result += jnp.dot(
@@ -388,14 +388,14 @@
     rest[-1][...] = (result * factor).astype(bf16)
 
 
-def output(blocks, state, start, gain, w_full, last):
+def output(blocks, steps, state, start, gain, w_full, last):
     count, rows, columns = w_full.shape
     heads, size, own = blocks[0].shape
     out_shape = [shape((own, columns), bf16)] if last else [
         shape((own, columns), f32), shape((1, own), f32)
     ]
     return call(
-        functools.partial(output_kernel, start * size, count * rows, state is None, last),
+        functools.partial(output_kernel, start * size, count * rows, steps, state is None, last),
         out_shape,
         [*blocks, gain.reshape(count, 1, rows), w_full, *(state or ())],
         flops=2 * own * count * heads * size * columns,
@@ -532,10 +532,14 @@
             level += 1
             sums = merge(level, got, *sums[1:])
         finished.append([partner(sums[s], "head", s) if s else sums[s] for s in range(head_count)])
+    jobs = [(n, tuple(range(head_count))) for n in range(len(CHUNKS))]
+    n, steps = jobs.pop()
+    jobs += [(n, steps[:1] + steps[2:]), (n, steps[1:2])]
     state = None
-    for n in range(len(CHUNKS)):
-        last = n + 1 == len(CHUNKS)
-        state = output(finished[n], state, starts[n], gain, w_full, last)
+    for i, (n, steps) in enumerate(jobs):
+        blocks = [finished[n][s] for s in steps]
+        last = i + 1 == len(jobs)
+        state = output(blocks, steps, state, starts[n], gain, w_full, last)
     return state[0]
 
 

time: 73.9 us -> 70.9 us (0.959)
  starting transfers between devices: 29.8 us -> 25.4 us
  waiting for transfers between devices: 25.2 us -> 26.4 us
    ppermute x23, starting transfers between devices: 29.8 us -> 25.4 us  [partner(): return lax.ppermute(value, axis, [(i, i ^ step) for i in range(count)])]
    ppermute x23, waiting for transfers between devices: 25.2 us -> 26.4 us  [partner(): return lax.ppermute(value, axis, [(i, i ^ step) for i in range(count)])]
    pallas_call x17 -> x18, Pallas kernels: 18.6 us -> 18.8 us  [call(): pl.pallas_call(kernel, out_shape=out_shape, in_specs=in_specs or [vmem] *...]
  transfers between devices with their start and end apart: 23 -> 23, of which waited for: 9 -> 8; matrix products, arithmetic and copies ran while one was open for 0% -> 0% of each run, Pallas kernels for 20% -> 22%
where the time goes in v1:
time: 70.9 us; the launch traced here: 70.8 us
  waiting for transfers between devices  26.4 us (37%)
  starting transfers between devices  25.4 us (36%)
  Pallas kernels  18.8 us (27%)
    ppermute x23, waiting for transfers between devices, partner(): return lax.ppermute(value, axis, [(i, i ^ step) for i in range(count)])  26.4 us
    ppermute x23, starting transfers between devices, partner(): return lax.ppermute(value, axis, [(i, i ^ step) for i in range(count)])  25.4 us
    pallas_call x18, Pallas kernels, call(): pl.pallas_call(kernel, out_shape=out_shape, in_specs=in_specs or [vmem] *...  18.8 us
  transfers between devices with their start and end apart: 23, of which 8 were waited for; matrix products, arithmetic and copies ran while one was open for 0% of the time, Pallas kernels for 22%

profile of v1, /device:TPU:0, one launch (start us, length us, event | category | flops | bytes accessed | tf_op | source)
XLA Modules:
  0.0 70.8 jit_solution(12829770876791705597)
XLA Ops:
  0.0 2.4 %shard_map.55 = (bf16[256,512]{1,0:T(8,128)(2,1)S(1)}, bf16[256,512]{1,0:T(8,128)(2,1)S(1)}, bf16[256,1024]{1,0:T(8,128)(2,1)S(1)}, bf16[32,1024]{1,0:T(8,128)(2,1)S(1)}) custom-call(bf16[256,1024]{1,0:T(8,128)(2,1)} %x_hbm.1, bf16[1024,2048]{1,0:T(8,128)(2,1)} %w_ref, bf16[256,1024]{1,0:T(8,128)(2,1)} %o_hbm.1), custom_call_target="tpu_custom_call" | custom-call | flops 536870912 | bytes 5242880 | tf_op jit(solution)/shard_map/pallas_call | solution.py:23
  2.5 3.1 %collective-permute-start.2 = (bf16[256,512]{1,0:T(8,128)(2,1)S(1)}, bf16[256,512]{1,0:T(8,128)(2,1)S(1)}, u32[]{:S(2)}, u32[]{:S(2)}) collective-permute-start(bf16[256,512]{1,0:T(8,128)(2,1)S(1)} %get-tuple-element.51), channel_id=1, source_target_pairs={{0,1},{1,0},{2,3},{3,2},{4,5},{5,4},{6,7},{7,6},{8,9},{9,8},{10,11... | collective-permute-start | bytes 786440 | tf_op jit(solution)/shard_map/ppermute | solution.py:42
  5.6 2.6 %collective-permute-start.6 = (bf16[1,32,1024]{2,1,0:T(8,128)(2,1)S(1)}, bf16[1,32,1024]{2,1,0:T(8,128)(2,1)S(1)}, u32[]{:S(2)}, u32[]{:S(2)}) collective-permute-start(bf16[1,32,1024]{2,1,0:T(8,128)(2,1)S(1)} %bitcast.2), channel_id=1, source_target_pairs={{0,2},{1,3},{2,0},{3,1},{4,6},{5,7},{6,4},{7,5},{8,10},{9,11},{10,... | collective-permute-start | bytes 196616 | tf_op jit(solution)/shard_map/ppermute | solution.py:42
  8.2 0.0 collective-permute-start.1
  8.2 5.6 %collective-permute-done.6.refs_1_ = bf16[1,32,1024]{2,1,0:T(8,128)(2,1)S(1)} collective-permute-done((bf16[1,32,1024]{2,1,0:T(8,128)(2,1)S(1)}, bf16[1,32,1024]{2,1,0:T(8,128)(2,1)S(1)}, u32[]{:S(2)}, u32[]{:S(2)}) %collective-permute-start.6) | collective-permute-done | bytes 65568 | tf_op jit(solution)/shard_map/ppermute | solution.py:42
  13.7 3.6 %collective-permute-start.7 = (bf16[2,32,1024]{2,1,0:T(8,128)(2,1)S(1)}, bf16[2,32,1024]{2,1,0:T(8,128)(2,1)S(1)}, u32[]{:S(2)}, u32[]{:S(2)}) collective-permute-start(bf16[2,32,1024]{2,1,0:T(8,128)(2,1)S(1)} %shard_map.64.refs_0_), channel_id=1, source_target_pairs={{0,1},{1,0},{2,3},{3,2},{4,5},{5,4},{6,7},{7,6},{8,9},{9,8},{10,11... | collective-permute-start | bytes 393224 | tf_op jit(solution)/shard_map/ppermute | solution.py:42
  17.3 0.0 copy-done
  17.4 0.7 %shard_map.57 = (bf16[256,512]{1,0:T(8,128)(2,1)S(1)}, bf16[256,256]{1,0:T(8,128)(2,1)S(1)}, bf16[256,256]{1,0:T(8,128)(2,1)S(1)}) custom-call(bf16[256,1024]{1,0:T(8,128)(2,1)S(1)} %get-tuple-element.47.x_ref, bf16[1024,2048]{1,0:T(8,128)(2,1)S(1)} %copy-done), custom_call_target="tpu_custom_call" | custom-call | flops 536870912 | bytes 4718592 | tf_op jit(solution)/shard_map/pallas_call | solution.py:23
  18.1 0.1 collective-permute-start.17
  18.2 2.9 %collective-permute-start = (bf16[256,256]{1,0:T(8,128)(2,1)S(1)}, bf16[256,256]{1,0:T(8,128)(2,1)S(1)}, u32[]{:S(2)}, u32[]{:S(2)}) collective-permute-start(bf16[256,256]{1,0:T(8,128)(2,1)S(1)} %get-tuple-element.49), channel_id=1, source_target_pairs={{0,2},{1,3},{2,0},{3,1},{4,6},{5,7},{6,4},{7,5},{8,10},{9,11},{10,... | collective-permute-start | bytes 393224 | tf_op jit(solution)/shard_map/ppermute | solution.py:42
  21.1 0.0 copy-done.1
  21.1 0.6 shard_map.56.q_ref
  21.7 2.4 %collective-permute-done.7.refs_1_ = bf16[2,32,1024]{2,1,0:T(8,128)(2,1)S(1)} collective-permute-done((bf16[2,32,1024]{2,1,0:T(8,128)(2,1)S(1)}, bf16[2,32,1024]{2,1,0:T(8,128)(2,1)S(1)}, u32[]{:S(2)}, u32[]{:S(2)}) %collective-permute-start.7) | collective-permute-done | bytes 131104 | tf_op jit(solution)/shard_map/ppermute | solution.py:42
  24.1 1.6 %collective-permute-start.8 = (bf16[4,32,1024]{2,1,0:T(8,128)(2,1)S(1)}, bf16[4,32,1024]{2,1,0:T(8,128)(2,1)S(1)}, u32[]{:S(2)}, u32[]{:S(2)}) collective-permute-start(bf16[4,32,1024]{2,1,0:T(8,128)(2,1)S(1)} %shard_map.65.refs_0_), channel_id=1, source_target_pairs={{0,8},{4,12},{8,0},{12,4},{1,9},{5,13},{9,1},{13,5},{2,10},{6,14},... | collective-permute-start | bytes 786440 | tf_op jit(solution)/shard_map/ppermute | solution.py:42
  25.6 2.9 %shard_map.58 = (f32[4,64,2048]{2,1,0:T(8,128)S(1)}, f32[4,2,2048]{2,1,0:T(2,128)S(1)}) custom-call(bf16[4,192,2048]{2,1,0:T(8,128)(2,1)S(1)} %shard_map.56.q_ref, bf16[256,512]{1,0:T(8,128)(2,1)S(1)} %get-tuple-element.52.rest_0_), custom_call_target="tpu_custom_call" | custom-call | flops 536870912 | bytes 3407872 | tf_op jit(solution)/shard_map/pallas_call | solution.py:23
  28.5 0.0 collective-permute-done.2.rest_0_
  28.6 3.0 %shard_map.59 = (f32[4,64,2048]{2,1,0:T(8,128)S(1)}, f32[4,2,2048]{2,1,0:T(2,128)S(1)}) custom-call(bf16[4,192,2048]{2,1,0:T(8,128)(2,1)S(1)} %shard_map.56.q_ref, bf16[256,512]{1,0:T(8,128)(2,1)S(1)} %collective-permute-done.2.rest_0_, f32[4,64,2048]{2,1,0:T(8,128)S(1)} %get-tuple-element.53.rest_1_, f32[4,2,2048]{2,1,0:T(2,128)S(1)} %get-tuple-element.54.rest_2_), custom_call_target="tpu_custom_call" | custom-call | flops 536870912 | bytes 5570560 | tf_op jit(solution)/shard_map/pallas_call | solution.py:23
  31.6 0.0 collective-permute-done.1.rest_0_
  31.6 3.0 %shard_map.60 = (f32[4,64,2048]{2,1,0:T(8,128)S(1)}, f32[4,2,2048]{2,1,0:T(2,128)S(1)}) custom-call(bf16[4,192,2048]{2,1,0:T(8,128)(2,1)S(1)} %shard_map.56.q_ref, bf16[256,512]{1,0:T(8,128)(2,1)S(1)} %collective-permute-done.1.rest_0_, f32[4,64,2048]{2,1,0:T(8,128)S(1)} %get-tuple-element.55.rest_1_, f32[4,2,2048]{2,1,0:T(2,128)S(1)} %get-tuple-element.56.rest_2_), custom_call_target="tpu_custom_call" | custom-call | flops 536870912 | bytes 5570560 | tf_op jit(solution)/shard_map/pallas_call | solution.py:23
  34.6 0.0 collective-permute-done.17.rest_0_
  34.6 1.7 %shard_map.67 = (bf16[2,72,1024]{2,1,0:T(8,128)(2,1)S(1)}, f32[2,64,1024]{2,1,0:T(8,128)S(1)}, f32[2,2,1024]{2,1,0:T(2,128)S(1)}) custom-call(bf16[4,192,2048]{2,1,0:T(8,128)(2,1)S(1)} %shard_map.56.q_ref, bf16[256,256]{1,0:T(8,128)(2,1)S(1)} %collective-permute-done.17.rest_0_, f32[4,64,2048]{2,1,0:T(8,128)S(1)} %get-tuple-element.57.rest_1_, ...), custom_call_target="tpu_custom_call" | custom-call | flops 268435456 | bytes 5439488 | tf_op jit(solution)/shard_map/pallas_call | solution.py:23
  36.3 0.1 collective-permute-start.18
  36.4 0.0 collective-permute-done.rest_0_
  36.4 1.9 %shard_map.61 = (bf16[2,72,1024]{2,1,0:T(8,128)(2,1)S(1)}, f32[2,64,1024]{2,1,0:T(8,128)S(1)}, f32[2,2,1024]{2,1,0:T(2,128)S(1)}) custom-call(bf16[4,192,2048]{2,1,0:T(8,128)(2,1)S(1)} %shard_map.56.q_ref, bf16[256,256]{1,0:T(8,128)(2,1)S(1)} %collective-permute-done.rest_0_, f32[4,64,2048]{2,1,0:T(8,128)S(1)} %get-tuple-element.57.rest_1_, ...), custom_call_target="tpu_custom_call" | custom-call | flops 268435456 | bytes 5439488 | tf_op jit(solution)/shard_map/pallas_call | solution.py:23
  38.2 0.6 collective-permute-start.3
  38.8 1.5 %collective-permute-start.9 = (bf16[4,32,1024]{2,1,0:T(8,128)(2,1)S(1)}, bf16[4,32,1024]{2,1,0:T(8,128)(2,1)S(1)}, u32[]{:S(2)}, u32[]{:S(2)}) collective-permute-start(bf16[4,32,1024]{2,1,0:T(8,128)(2,1)S(1)} %shard_map.65.refs_0_), channel_id=1, source_target_pairs={{0,16},{16,0},{1,17},{17,1},{2,18},{18,2},{3,19},{19,3},{4,20},{20... | collective-permute-start | bytes 786440 | tf_op jit(solution)/shard_map/ppermute | solution.py:42
  40.3 0.0 collective-permute-done.8.refs_1_
  40.3 0.5 collective-permute-start.10
  40.8 0.0 collective-permute-done.18.got_ref
  40.8 0.2 shard_map.68
  41.0 0.6 collective-permute-start.19
  41.6 0.0 collective-permute-start.11
  41.6 6.4 %collective-permute-done.9.refs_2_ = bf16[4,32,1024]{2,1,0:T(8,128)(2,1)S(1)} collective-permute-done((bf16[4,32,1024]{2,1,0:T(8,128)(2,1)S(1)}, bf16[4,32,1024]{2,1,0:T(8,128)(2,1)S(1)}, u32[]{:S(2)}, u32[]{:S(2)}) %collective-permute-start.9) | collective-permute-done | bytes 262176 | tf_op jit(solution)/shard_map/ppermute | solution.py:42
  48.0 0.0 collective-permute-start.12
  48.0 0.0 collective-permute-done.3.got_ref
  48.0 0.5 collective-permute-start.13
  48.5 4.2 %collective-permute-done.10.refs_3_ = bf16[4,32,1024]{2,1,0:T(8,128)(2,1)S(1)} collective-permute-done((bf16[4,32,1024]{2,1,0:T(8,128)(2,1)S(1)}, bf16[4,32,1024]{2,1,0:T(8,128)(2,1)S(1)}, u32[]{:S(2)}, u32[]{:S(2)}) %collective-permute-start.10) | collective-permute-done | bytes 262176 | tf_op jit(solution)/shard_map/ppermute | solution.py:42
  52.7 0.0 collective-permute-start.14
  52.7 0.2 shard_map.62
  52.9 0.0 collective-permute-done.19.got_ref
  52.9 0.6 collective-permute-start.4
  53.5 0.1 shard_map.69
  53.6 0.0 collective-permute-done.11.refs_4_
  53.6 0.7 collective-permute-start.20
  54.2 5.0 %collective-permute-done.4.got_ref = bf16[2,72,512]{2,1,0:T(8,128)(2,1)S(1)} collective-permute-done((bf16[2,72,512]{2,1,0:T(8,128)(2,1)S(1)}, bf16[2,72,512]{2,1,0:T(8,128)(2,1)S(1)}, u32[]{:S(2)}, u32[]{:S(2)}) %collective-permute-start.4) | collective-permute-done | bytes 147488 | tf_op jit(solution)/shard_map/ppermute | solution.py:42
  59.2 1.6 %collective-permute-start.21 = (bf16[2,64,128]{2,1,0:T(8,128)(2,1)S(1)}, bf16[2,64,128]{2,1,0:T(8,128)(2,1)S(1)}, u32[]{:S(2)}, u32[]{:S(2)}) collective-permute-start(bf16[2,64,128]{2,1,0:T(8,128)(2,1)S(1)} %get-tuple-element.79), channel_id=1, source_target_pairs={{0,2},{1,3},{2,0},{3,1},{4,6},{5,7},{6,4},{7,5},{8,10},{9,11},{10,... | collective-permute-start | bytes 98312 | tf_op jit(solution)/shard_map/ppermute | solution.py:42
  60.8 0.0 collective-permute-done.12.refs_5_
  60.8 1.3 %collective-permute-start.22 = (bf16[2,64,128]{2,1,0:T(8,128)(2,1)S(1)}, bf16[2,64,128]{2,1,0:T(8,128)(2,1)S(1)}, u32[]{:S(2)}, u32[]{:S(2)}) collective-permute-start(bf16[2,64,128]{2,1,0:T(8,128)(2,1)S(1)} %get-tuple-element.80), channel_id=1, source_target_pairs={{0,3},{1,2},{2,1},{3,0},{4,7},{5,6},{6,5},{7,4},{8,11},{9,10},{10,... | collective-permute-start | bytes 98312 | tf_op jit(solution)/shard_map/ppermute | solution.py:42
  62.2 0.1 shard_map.63
  62.3 0.0 collective-permute-done.13.refs_6_
  62.3 1.3 %collective-permute-start.15 = (bf16[2,64,128]{2,1,0:T(8,128)(2,1)S(1)}, bf16[2,64,128]{2,1,0:T(8,128)(2,1)S(1)}, u32[]{:S(2)}, u32[]{:S(2)}) collective-permute-start(bf16[2,64,128]{2,1,0:T(8,128)(2,1)S(1)} %get-tuple-element.68), channel_id=1, source_target_pairs={{0,2},{1,3},{2,0},{3,1},{4,6},{5,7},{6,4},{7,5},{8,10},{9,11},{10,... | collective-permute-start | bytes 98312 | tf_op jit(solution)/shard_map/ppermute | solution.py:42
  63.5 0.0 collective-permute-done.20.refs_1_
  63.6 1.7 %collective-permute-start.16 = (bf16[2,64,128]{2,1,0:T(8,128)(2,1)S(1)}, bf16[2,64,128]{2,1,0:T(8,128)(2,1)S(1)}, u32[]{:S(2)}, u32[]{:S(2)}) collective-permute-start(bf16[2,64,128]{2,1,0:T(8,128)(2,1)S(1)} %get-tuple-element.69), channel_id=1, source_target_pairs={{0,3},{1,2},{2,1},{3,0},{4,7},{5,6},{6,5},{7,4},{8,11},{9,10},{10,... | collective-permute-start | bytes 98312 | tf_op jit(solution)/shard_map/ppermute | solution.py:42
  65.2 0.0 collective-permute-done.14.refs_7_
  65.2 0.6 collective-permute-start.5
  65.8 0.2 shard_map.66.refs_5_.refs_4_.refs_2_
  66.0 0.0 collective-permute-done.21.refs_2_
  66.0 0.6 collective-permute-done.22.refs_3_
  66.6 0.5 shard_map.70
  67.1 0.9 %collective-permute-done.15.refs_1_ = bf16[2,64,128]{2,1,0:T(8,128)(2,1)S(1)} collective-permute-done((bf16[2,64,128]{2,1,0:T(8,128)(2,1)S(1)}, bf16[2,64,128]{2,1,0:T(8,128)(2,1)S(1)}, u32[]{:S(2)}, u32[]{:S(2)}) %collective-permute-start.15) | collective-permute-done | bytes 32800 | tf_op jit(solution)/shard_map/ppermute | solution.py:42
  67.9 1.4 %collective-permute-done.16.refs_2_ = bf16[2,64,128]{2,1,0:T(8,128)(2,1)S(1)} collective-permute-done((bf16[2,64,128]{2,1,0:T(8,128)(2,1)S(1)}, bf16[2,64,128]{2,1,0:T(8,128)(2,1)S(1)}, u32[]{:S(2)}, u32[]{:S(2)}) %collective-permute-start.16) | collective-permute-done | bytes 32800 | tf_op jit(solution)/shard_map/ppermute | solution.py:42
  69.4 0.4 shard_map.71
  69.8 0.0 collective-permute-done.5.refs_0_
  69.8 1.0 %shard_map.72 = bf16[128,1024]{1,0:T(8,128)(2,1)} custom-call(bf16[2,64,128]{2,1,0:T(8,128)(2,1)S(1)} %collective-permute-done.5.refs_0_, f32[4,1,256]{2,1,0:T(1,128)S(1)} %bitcast.6, bf16[4,256,1024]{2,1,0:T(8,128)(2,1)S(1)} %shard_map.66.refs_5_.refs_4_.refs_2_, f32[128,1024]{1,0:T(8,128)S(1)} %get-tuple-element.83.refs_3_, ...), custom_call_target="tpu_custom_call" | custom-call | flops 134217728 | bytes 2658816 | tf_op jit(solution)/shard_map/pallas_call | solution.py:23
  (6 shorter events, 0.0 us)
Async XLA Ops:
  0.0 17.3 %copy-start = (bf16[1024,2048]{1,0:T(8,128)(2,1)S(1)}, bf16[1024,2048]{1,0:T(8,128)(2,1)}, u32[]{:S(2)}) copy-start(bf16[1024,2048]{1,0:T(8,128)(2,1)} %w_ref) | copy-start | bytes 12582916
  2.5 26.1 %collective-permute-start.2 = (bf16[256,512]{1,0:T(8,128)(2,1)S(1)}, bf16[256,512]{1,0:T(8,128)(2,1)S(1)}, u32[]{:S(2)}, u32[]{:S(2)}) collective-permute-start(bf16[256,512]{1,0:T(8,128)(2,1)S(1)} %get-tuple-element.51), channel_id=1, source_target_pairs={{0,1},{1,0},{2,3},{3,2},{4,5},{5,4},{6,7},{7,6},{8,9},{9,8},{10,11... | collective-permute-start | bytes 786440 | tf_op jit(solution)/shard_map/ppermute | solution.py:42
  5.6 8.1 %collective-permute-start.6 = (bf16[1,32,1024]{2,1,0:T(8,128)(2,1)S(1)}, bf16[1,32,1024]{2,1,0:T(8,128)(2,1)S(1)}, u32[]{:S(2)}, u32[]{:S(2)}) collective-permute-start(bf16[1,32,1024]{2,1,0:T(8,128)(2,1)S(1)} %bitcast.2), channel_id=1, source_target_pairs={{0,2},{1,3},{2,0},{3,1},{4,6},{5,7},{6,4},{7,5},{8,10},{9,11},{10,... | collective-permute-start | bytes 196616 | tf_op jit(solution)/shard_map/ppermute | solution.py:42
  8.2 23.4 %collective-permute-start.1 = (bf16[256,512]{1,0:T(8,128)(2,1)S(1)}, bf16[256,512]{1,0:T(8,128)(2,1)S(1)}, u32[]{:S(2)}, u32[]{:S(2)}) collective-permute-start(bf16[256,512]{1,0:T(8,128)(2,1)S(1)} %get-tuple-element.50), channel_id=1, source_target_pairs={{0,3},{1,2},{2,1},{3,0},{4,7},{5,6},{6,5},{7,4},{8,11},{9,10},{10,... | collective-permute-start | bytes 786440 | tf_op jit(solution)/shard_map/ppermute | solution.py:42
  13.7 10.3 %collective-permute-start.7 = (bf16[2,32,1024]{2,1,0:T(8,128)(2,1)S(1)}, bf16[2,32,1024]{2,1,0:T(8,128)(2,1)S(1)}, u32[]{:S(2)}, u32[]{:S(2)}) collective-permute-start(bf16[2,32,1024]{2,1,0:T(8,128)(2,1)S(1)} %shard_map.64.refs_0_), channel_id=1, source_target_pairs={{0,1},{1,0},{2,3},{3,2},{4,5},{5,4},{6,7},{7,6},{8,9},{9,8},{10,11... | collective-permute-start | bytes 393224 | tf_op jit(solution)/shard_map/ppermute | solution.py:42
  17.3 3.7 %copy-start.1 = (bf16[4,64,2048]{2,1,0:T(8,128)(2,1)S(1)}, bf16[4,64,2048]{2,1,0:T(8,128)(2,1)}, u32[]{:S(2)}) copy-start(bf16[4,64,2048]{2,1,0:T(8,128)(2,1)} %q_ref) | copy-start | bytes 3145732
  18.1 16.6 %collective-permute-start.17 = (bf16[256,256]{1,0:T(8,128)(2,1)S(1)}, bf16[256,256]{1,0:T(8,128)(2,1)S(1)}, u32[]{:S(2)}, u32[]{:S(2)}) collective-permute-start(bf16[256,256]{1,0:T(8,128)(2,1)S(1)} %get-tuple-element.70), channel_id=1, source_target_pairs={{0,2},{1,3},{2,0},{3,1},{4,6},{5,7},{6,4},{7,5},{8,10},{9,11},{10,... | collective-permute-start | bytes 393224 | tf_op jit(solution)/shard_map/ppermute | solution.py:42
  18.2 18.2 %collective-permute-start = (bf16[256,256]{1,0:T(8,128)(2,1)S(1)}, bf16[256,256]{1,0:T(8,128)(2,1)S(1)}, u32[]{:S(2)}, u32[]{:S(2)}) collective-permute-start(bf16[256,256]{1,0:T(8,128)(2,1)S(1)} %get-tuple-element.49), channel_id=1, source_target_pairs={{0,2},{1,3},{2,0},{3,1},{4,6},{5,7},{6,4},{7,5},{8,10},{9,11},{10,... | collective-permute-start | bytes 393224 | tf_op jit(solution)/shard_map/ppermute | solution.py:42
  24.1 16.2 %collective-permute-start.8 = (bf16[4,32,1024]{2,1,0:T(8,128)(2,1)S(1)}, bf16[4,32,1024]{2,1,0:T(8,128)(2,1)S(1)}, u32[]{:S(2)}, u32[]{:S(2)}) collective-permute-start(bf16[4,32,1024]{2,1,0:T(8,128)(2,1)S(1)} %shard_map.65.refs_0_), channel_id=1, source_target_pairs={{0,8},{4,12},{8,0},{12,4},{1,9},{5,13},{9,1},{13,5},{2,10},{6,14},... | collective-permute-start | bytes 786440 | tf_op jit(solution)/shard_map/ppermute | solution.py:42
  36.3 4.5 %collective-permute-start.18 = (bf16[2,72,1024]{2,1,0:T(8,128)(2,1)S(1)}, bf16[2,72,1024]{2,1,0:T(8,128)(2,1)S(1)}, u32[]{:S(2)}, u32[]{:S(2)}) collective-permute-start(bf16[2,72,1024]{2,1,0:T(8,128)(2,1)S(1)} %get-tuple-element.71), channel_id=1, source_target_pairs={{0,4},{4,0},{8,12},{12,8},{1,5},{5,1},{9,13},{13,9},{2,6},{6,2},{1... | collective-permute-start | bytes 884744 | tf_op jit(solution)/shard_map/ppermute | solution.py:42
  38.2 9.7 %collective-permute-start.3 = (bf16[2,72,1024]{2,1,0:T(8,128)(2,1)S(1)}, bf16[2,72,1024]{2,1,0:T(8,128)(2,1)S(1)}, u32[]{:S(2)}, u32[]{:S(2)}) collective-permute-start(bf16[2,72,1024]{2,1,0:T(8,128)(2,1)S(1)} %get-tuple-element.59), channel_id=1, source_target_pairs={{0,4},{4,0},{8,12},{12,8},{1,5},{5,1},{9,13},{13,9},{2,6},{6,2},{1... | collective-permute-start | bytes 884744 | tf_op jit(solution)/shard_map/ppermute | solution.py:42
  38.8 9.2 %collective-permute-start.9 = (bf16[4,32,1024]{2,1,0:T(8,128)(2,1)S(1)}, bf16[4,32,1024]{2,1,0:T(8,128)(2,1)S(1)}, u32[]{:S(2)}, u32[]{:S(2)}) collective-permute-start(bf16[4,32,1024]{2,1,0:T(8,128)(2,1)S(1)} %shard_map.65.refs_0_), channel_id=1, source_target_pairs={{0,16},{16,0},{1,17},{17,1},{2,18},{18,2},{3,19},{19,3},{4,20},{20... | collective-permute-start | bytes 786440 | tf_op jit(solution)/shard_map/ppermute | solution.py:42
  40.3 12.4 %collective-permute-start.10 = (bf16[4,32,1024]{2,1,0:T(8,128)(2,1)S(1)}, bf16[4,32,1024]{2,1,0:T(8,128)(2,1)S(1)}, u32[]{:S(2)}, u32[]{:S(2)}) collective-permute-start(bf16[4,32,1024]{2,1,0:T(8,128)(2,1)S(1)} %collective-permute-done.8.refs_1_), channel_id=1, source_target_pairs={{0,16},{16,0},{1,17},{17,1},{2,18},{18,2},{3,19},{19,3},{4,20},{20... | collective-permute-start | bytes 786440 | tf_op jit(solution)/shard_map/ppermute | solution.py:42
  41.0 11.9 %collective-permute-start.19 = (bf16[2,72,512]{2,1,0:T(8,128)(2,1)S(1)}, bf16[2,72,512]{2,1,0:T(8,128)(2,1)S(1)}, u32[]{:S(2)}, u32[]{:S(2)}) collective-permute-start(bf16[2,72,512]{2,1,0:T(8,128)(2,1)S(1)} %get-tuple-element.74), channel_id=1, source_target_pairs={{0,8},{4,12},{8,0},{12,4},{1,9},{5,13},{9,1},{13,5},{2,10},{6,14},... | collective-permute-start | bytes 442376 | tf_op jit(solution)/shard_map/ppermute | solution.py:42
  41.6 12.0 %collective-permute-start.11 = (bf16[4,32,1024]{2,1,0:T(8,128)(2,1)S(1)}, bf16[4,32,1024]{2,1,0:T(8,128)(2,1)S(1)}, u32[]{:S(2)}, u32[]{:S(2)}) collective-permute-start(bf16[4,32,1024]{2,1,0:T(8,128)(2,1)S(1)} %shard_map.65.refs_0_), channel_id=1, source_target_pairs={{0,4},{4,0},{8,12},{12,8},{1,5},{5,1},{9,13},{13,9},{2,6},{6,2},{1... | collective-permute-start | bytes 786440 | tf_op jit(solution)/shard_map/ppermute | solution.py:42
  48.0 12.9 %collective-permute-start.12 = (bf16[4,32,1024]{2,1,0:T(8,128)(2,1)S(1)}, bf16[4,32,1024]{2,1,0:T(8,128)(2,1)S(1)}, u32[]{:S(2)}, u32[]{:S(2)}) collective-permute-start(bf16[4,32,1024]{2,1,0:T(8,128)(2,1)S(1)} %collective-permute-done.8.refs_1_), channel_id=1, source_target_pairs={{0,4},{4,0},{8,12},{12,8},{1,5},{5,1},{9,13},{13,9},{2,6},{6,2},{1... | collective-permute-start | bytes 786440 | tf_op jit(solution)/shard_map/ppermute | solution.py:42
  48.0 14.3 %collective-permute-start.13 = (bf16[4,32,1024]{2,1,0:T(8,128)(2,1)S(1)}, bf16[4,32,1024]{2,1,0:T(8,128)(2,1)S(1)}, u32[]{:S(2)}, u32[]{:S(2)}) collective-permute-start(bf16[4,32,1024]{2,1,0:T(8,128)(2,1)S(1)} %collective-permute-done.9.refs_2_), channel_id=1, source_target_pairs={{0,4},{4,0},{8,12},{12,8},{1,5},{5,1},{9,13},{13,9},{2,6},{6,2},{1... | collective-permute-start | bytes 786440 | tf_op jit(solution)/shard_map/ppermute | solution.py:42
  52.7 12.5 %collective-permute-start.14 = (bf16[4,32,1024]{2,1,0:T(8,128)(2,1)S(1)}, bf16[4,32,1024]{2,1,0:T(8,128)(2,1)S(1)}, u32[]{:S(2)}, u32[]{:S(2)}) collective-permute-start(bf16[4,32,1024]{2,1,0:T(8,128)(2,1)S(1)} %collective-permute-done.10.refs_3_), channel_id=1, source_target_pairs={{0,4},{4,0},{8,12},{12,8},{1,5},{5,1},{9,13},{13,9},{2,6},{6,2},{1... | collective-permute-start | bytes 786440 | tf_op jit(solution)/shard_map/ppermute | solution.py:42
  52.9 6.3 %collective-permute-start.4 = (bf16[2,72,512]{2,1,0:T(8,128)(2,1)S(1)}, bf16[2,72,512]{2,1,0:T(8,128)(2,1)S(1)}, u32[]{:S(2)}, u32[]{:S(2)}) collective-permute-start(bf16[2,72,512]{2,1,0:T(8,128)(2,1)S(1)} %get-tuple-element.62), channel_id=1, source_target_pairs={{0,8},{4,12},{8,0},{12,4},{1,9},{5,13},{9,1},{13,5},{2,10},{6,14},... | collective-permute-start | bytes 442376 | tf_op jit(solution)/shard_map/ppermute | solution.py:42
  53.6 10.0 %collective-permute-start.20 = (bf16[2,64,128]{2,1,0:T(8,128)(2,1)S(1)}, bf16[2,64,128]{2,1,0:T(8,128)(2,1)S(1)}, u32[]{:S(2)}, u32[]{:S(2)}) collective-permute-start(bf16[2,64,128]{2,1,0:T(8,128)(2,1)S(1)} %get-tuple-element.78), channel_id=1, source_target_pairs={{0,1},{1,0},{2,3},{3,2},{4,5},{5,4},{6,7},{7,6},{8,9},{9,8},{10,11... | collective-permute-start | bytes 98312 | tf_op jit(solution)/shard_map/ppermute | solution.py:42
  59.2 6.8 %collective-permute-start.21 = (bf16[2,64,128]{2,1,0:T(8,128)(2,1)S(1)}, bf16[2,64,128]{2,1,0:T(8,128)(2,1)S(1)}, u32[]{:S(2)}, u32[]{:S(2)}) collective-permute-start(bf16[2,64,128]{2,1,0:T(8,128)(2,1)S(1)} %get-tuple-element.79), channel_id=1, source_target_pairs={{0,2},{1,3},{2,0},{3,1},{4,6},{5,7},{6,4},{7,5},{8,10},{9,11},{10,... | collective-permute-start | bytes 98312 | tf_op jit(solution)/shard_map/ppermute | solution.py:42
  60.8 5.7 %collective-permute-start.22 = (bf16[2,64,128]{2,1,0:T(8,128)(2,1)S(1)}, bf16[2,64,128]{2,1,0:T(8,128)(2,1)S(1)}, u32[]{:S(2)}, u32[]{:S(2)}) collective-permute-start(bf16[2,64,128]{2,1,0:T(8,128)(2,1)S(1)} %get-tuple-element.80), channel_id=1, source_target_pairs={{0,3},{1,2},{2,1},{3,0},{4,7},{5,6},{6,5},{7,4},{8,11},{9,10},{10,... | collective-permute-start | bytes 98312 | tf_op jit(solution)/shard_map/ppermute | solution.py:42
  62.3 5.7 %collective-permute-start.15 = (bf16[2,64,128]{2,1,0:T(8,128)(2,1)S(1)}, bf16[2,64,128]{2,1,0:T(8,128)(2,1)S(1)}, u32[]{:S(2)}, u32[]{:S(2)}) collective-permute-start(bf16[2,64,128]{2,1,0:T(8,128)(2,1)S(1)} %get-tuple-element.68), channel_id=1, source_target_pairs={{0,2},{1,3},{2,0},{3,1},{4,6},{5,7},{6,4},{7,5},{8,10},{9,11},{10,... | collective-permute-start | bytes 98312 | tf_op jit(solution)/shard_map/ppermute | solution.py:42
  63.6 5.8 %collective-permute-start.16 = (bf16[2,64,128]{2,1,0:T(8,128)(2,1)S(1)}, bf16[2,64,128]{2,1,0:T(8,128)(2,1)S(1)}, u32[]{:S(2)}, u32[]{:S(2)}) collective-permute-start(bf16[2,64,128]{2,1,0:T(8,128)(2,1)S(1)} %get-tuple-element.69), channel_id=1, source_target_pairs={{0,3},{1,2},{2,1},{3,0},{4,7},{5,6},{6,5},{7,4},{8,11},{9,10},{10,... | collective-permute-start | bytes 98312 | tf_op jit(solution)/shard_map/ppermute | solution.py:42
  65.2 1.4 %copy-start.2 = (f32[1024]{0:T(1024)S(1)}, f32[1024]{0:T(1024)}, u32[]{:S(2)}) copy-start(f32[1024]{0:T(1024)} %param.8) | copy-start | bytes 12292
  65.2 4.6 %collective-permute-start.5 = (bf16[2,64,128]{2,1,0:T(8,128)(2,1)S(1)}, bf16[2,64,128]{2,1,0:T(8,128)(2,1)S(1)}, u32[]{:S(2)}, u32[]{:S(2)}) collective-permute-start(bf16[2,64,128]{2,1,0:T(8,128)(2,1)S(1)} %get-tuple-element.65), channel_id=1, source_target_pairs={{0,1},{1,0},{2,3},{3,2},{4,5},{5,4},{6,7},{7,6},{8,9},{9,8},{10,11... | collective-permute-start | bytes 98312 | tf_op jit(solution)/shard_map/ppermute | solution.py:42
